TPU v7x, 32 devices: a whole 2x2x4 slice. The times are simulated.
32 devices in a mesh: dp: 8 (over z, x), tensor: 4 (over y, core).
Axes of the slice: x: 2, y: 2, z: 4, core: 2. Of those that a mesh axis runs over, the one named last changes fastest.
Arguments:
- hidden_in: bfloat16 [10240, 2048], P(('dp', 'tensor')), may hold values from -6 to 6
- skip_mask: int32 [10240], P(('dp', 'tensor')), may hold values 0 or 1
- parents: int32 [8, 10], P('dp'), may hold values from 0 to 5, as said below
- attention_gain: bfloat16 [2048], P('dp'), may hold values from 0.099609375 to 1.8984375
- query_weight: bfloat16 [2048, 2048], P('dp', 'tensor'), may hold values from -0.25 to 0.25
- key_weight: bfloat16 [2048, 512], P('dp', 'tensor'), may hold values from -0.125 to 0.125
- value_weight: bfloat16 [2048, 512], P('dp', 'tensor'), may hold values from -0.125 to 0.125
- output_weight: bfloat16 [2048, 2048], P('dp', 'tensor'), may hold values from -0.5 to 0.5
- feedforward_gain: bfloat16 [2048], P('dp'), may hold values from 0.099609375 to 1.8984375
- gate_weight: bfloat16 [2048, 5632], P('dp', 'tensor'), may hold values from -0.125 to 0.125
- up_weight: bfloat16 [2048, 5632], P('dp', 'tensor'), may hold values from -0.125 to 0.125
- down_weight: bfloat16 [2048, 5632], P('dp', 'tensor'), may hold values from -0.15625 to 0.15625
- grad_out: bfloat16 [10240, 2048], P(('dp', 'tensor')), may hold values from -6 to 6
Outputs:
- layer_out: bfloat16 [10240, 2048], P(('dp', 'tensor'))
- input_grad: float32 [10240, 2048], P(('dp', 'tensor'))
- grad_attention_gain: float32 [2048], P('dp')
- grad_query_weight: float32 [2048, 2048], P('dp', 'tensor')
- grad_key_weight: float32 [2048, 512], P('dp', 'tensor')
- grad_value_weight: float32 [2048, 512], P('dp', 'tensor')
- grad_output_weight: float32 [2048, 2048], P('dp', 'tensor')
- grad_feedforward_gain: float32 [2048], P('dp')
- grad_gate_weight: float32 [2048, 5632], P('dp', 'tensor')
- grad_up_weight: float32 [2048, 5632], P('dp', 'tensor')
- grad_down_weight: float32 [2048, 5632], P('dp', 'tensor')
Inputs may be any that keep to these rules, and one draw needn't show every extreme that they name: `parents`: in every tree, blocks 0 to 3 form a chain (block 0 is its own parent, block b has parent b - 1); the next 2 blocks have parent 4 - 1; each of the last 4 blocks has one of those 2 blocks as parent, and each of those 2 blocks is parent of exactly 2 of the last 4 blocks.
All inputs are finite; a program needn't handle non-finite values. No bound on the sum of `skip_mask` on one device may be relied on, other than what follows from the above.
Results may differ from a plain program's by a relative error of at most 0.023.
Values may be sent and summed in bfloat16 or wider, within the bound.
No kernel may reach another device: no remote copies, remote signals or barrier semaphores. Data moves between devices by JAX's collectives and lax.ppermute only.
A program may use at most 192 MiB of HBM per device.

v0:
```python
import math
import jax
import jax.numpy as jnp
from jax import lax
from jax.sharding import PartitionSpec as P

HD = 128
epsilon = 1e-05
masked_score = -1000000000.0


def tree_layout(parent_ids):
    count = parent_ids.shape[0]
    blocks = jnp.arange(count, dtype=jnp.int32)
    ancestor = blocks[:, None] == blocks[None, :]
    current = blocks
    for sweep in range(count):
        current = jnp.sum(
            jnp.where(blocks[None, :] == current[:, None], parent_ids[None, :], 0), axis=1
        )
        ancestor = ancestor | (blocks[None, :] == current[:, None])
    depth = jnp.sum(ancestor.astype(jnp.int32), axis=1) - 1
    return (ancestor, depth)


def tree_tables(ancestor, depth, block_len, head_size):
    count = depth.shape[0]
    length = count * block_len
    visible = jnp.broadcast_to(
        ancestor[:, None, :, None], (count, block_len, count, block_len)
    ).reshape(length, length)
    places = jnp.arange(length, dtype=jnp.int32)
    block_of = places // block_len
    later = (block_of[:, None] == block_of[None, :]) & (places[None, :] > places[:, None])
    allowed = visible & jnp.logical_not(later)
    block_ids = jnp.arange(count, dtype=jnp.int32)
    row_depth = jnp.sum(
        jnp.where(block_of[:, None] == block_ids[None, :], depth[None, :], 0), axis=1
    )
    position = (row_depth * block_len + places % block_len).astype(jnp.float32)
    half_size = head_size // 2
    freqs = jnp.exp(
        jnp.arange(half_size, dtype=jnp.float32) * (-2.0 * math.log(10000.0) / head_size)
    )
    angles = position[:, None] * freqs[None, :]
    cosine = jnp.concatenate([jnp.cos(angles), jnp.cos(angles)], axis=1)[:, None, :]
    sine = jnp.concatenate([jnp.sin(angles), jnp.sin(angles)], axis=1)[:, None, :]
    return (allowed, cosine, sine)


def rotate(values_in, cosine, sine):
    half_size = values_in.shape[-1] // 2
    turned = jnp.concatenate([-values_in[..., half_size:], values_in[..., :half_size]], axis=-1)
    return values_in * cosine + turned * sine


def rotate_back(grads_in, cosine, sine):
    half_size = grads_in.shape[-1] // 2
    scaled = grads_in * sine
    return grads_in * cosine + jnp.concatenate(
        [scaled[..., half_size:], -scaled[..., :half_size]], axis=-1
    )


def rms_scale(values_in):
    return lax.rsqrt(jnp.mean(values_in * values_in, axis=-1, keepdims=True) + epsilon)


def body(
    hidden_in,
    skip_mask,
    parents,
    attention_gain,
    query_weight,
    key_weight,
    value_weight,
    output_weight,
    feedforward_gain,
    gate_weight,
    up_weight,
    down_weight,
    grad_out,
):
    local_rows = hidden_in.shape[0]
    length = local_rows * lax.axis_size("tensor")
    parent_ids = parents[0]
    block_len = length // parent_ids.shape[0]
    ancestor, depth = tree_layout(parent_ids)
    allowed, cosine, sine = tree_tables(ancestor, depth, block_len, HD)
    keep = (1 - skip_mask).astype(jnp.float32)[:, None]

    def attention_weights():
        return (
            lax.all_gather(attention_gain, "dp", axis=0, tiled=True),
            lax.all_gather(query_weight, "dp", axis=0, tiled=True),
            lax.all_gather(key_weight, "dp", axis=0, tiled=True),
            lax.all_gather(value_weight, "dp", axis=0, tiled=True),
            lax.all_gather(output_weight, "dp", axis=0, tiled=True),
        )

    def feedforward_weights():
        return (
            lax.all_gather(feedforward_gain, "dp", axis=0, tiled=True),
            lax.all_gather(gate_weight, "dp", axis=0, tiled=True),
            lax.all_gather(up_weight, "dp", axis=0, tiled=True),
            lax.all_gather(down_weight, "dp", axis=0, tiled=True),
        )

    def gain_total(partial_sum):
        return lax.psum(partial_sum, "tensor")

    gain_one, weight_query, weight_key, weight_value, weight_output = attention_weights()
    inputs = hidden_in.astype(jnp.float32)
    scale_one = rms_scale(inputs)
    unit_one = inputs * scale_one
    normed = (unit_one * gain_one.astype(jnp.float32)).astype(jnp.bfloat16)
    normed_all = lax.all_gather(normed, "tensor", axis=0, tiled=True)
    heads_dev = weight_query.shape[1] // HD
    kv_dev = weight_key.shape[1] // HD
    group = heads_dev // kv_dev
    scale = HD ** (-0.5)
    half_len = length // 2
    items = heads_dev * 2
    query_raw = jnp.dot(normed_all, weight_query, preferred_element_type=jnp.float32).reshape(
        length, heads_dev, HD
    )
    key_raw = jnp.dot(normed_all, weight_key, preferred_element_type=jnp.float32).reshape(
        length, kv_dev, HD
    )
    values_all = jnp.dot(normed_all, weight_value, preferred_element_type=jnp.float32).astype(
        jnp.bfloat16
    )
    queries = rotate(query_raw, cosine, sine).astype(jnp.bfloat16)
    keys_rot = rotate(key_raw, cosine, sine).astype(jnp.bfloat16)
    query_items = queries.transpose(1, 0, 2).reshape(items, half_len, HD)
    key_heads = keys_rot.transpose(1, 0, 2)
    value_heads = values_all.reshape(length, kv_dev, HD).transpose(1, 0, 2)
    item_ids = jnp.arange(items, dtype=jnp.int32)

    def item_scores(query_block, item):
        kv_index = item // 2 // group
        key_block = lax.dynamic_index_in_dim(key_heads, kv_index, 0, keepdims=False)
        value_block = lax.dynamic_index_in_dim(value_heads, kv_index, 0, keepdims=False)
        mask_rows = lax.dynamic_slice_in_dim(allowed, item % 2 * half_len, half_len, 0)
        scores = (
            jnp.einsum("rd,md->rm", query_block, key_block, preferred_element_type=jnp.float32)
            * scale
        )
        return (jnp.where(mask_rows, scores, masked_score), key_block, value_block)

    def attend_item(operands):
        query_block, item = operands
        scores, key_block, value_block = item_scores(query_block, item)
        top = jnp.max(scores, axis=-1, keepdims=True)
        weights_raw = jnp.exp(scores - top)
        total = jnp.sum(weights_raw, axis=-1, keepdims=True)
        probs = weights_raw / total
        mixed_block = jnp.dot(
            probs.astype(jnp.bfloat16), value_block, preferred_element_type=jnp.float32
        ).astype(jnp.bfloat16)
        return (mixed_block, (top + jnp.log(total))[:, 0])

    mixed_items, log_totals = lax.map(attend_item, (query_items, item_ids))
    mixed = (
        mixed_items.reshape(heads_dev, length, HD)
        .transpose(1, 0, 2)
        .reshape(length, heads_dev * HD)
    )
    attended = lax.psum_scatter(
        jnp.einsum("lc,dc->ld", mixed, weight_output, preferred_element_type=jnp.float32),
        "tensor",
        scatter_dimension=0,
        tiled=True,
    )
    middle = inputs + keep * attended
    gain_two, weight_gate, weight_up, weight_down = feedforward_weights()
    scale_two = rms_scale(middle)
    unit_two = middle * scale_two
    normed_ff = (unit_two * gain_two.astype(jnp.float32)).astype(jnp.bfloat16)
    normed_ff_all = lax.all_gather(normed_ff, "tensor", axis=0, tiled=True)
    gate = jnp.dot(normed_ff_all, weight_gate, preferred_element_type=jnp.float32)
    upward = jnp.dot(normed_ff_all, weight_up, preferred_element_type=jnp.float32)
    sigma = jax.nn.sigmoid(gate)
    active = gate * sigma
    hidden_ff = (active * upward).astype(jnp.bfloat16)
    branch = lax.psum_scatter(
        jnp.einsum("lf,df->ld", hidden_ff, weight_down, preferred_element_type=jnp.float32).astype(
            jnp.bfloat16
        ),
        "tensor",
        scatter_dimension=0,
        tiled=True,
    ).astype(jnp.float32)
    layer_out = (middle + keep * branch).astype(jnp.bfloat16)
    cotangent = grad_out.astype(jnp.float32)
    gain_two, weight_gate, weight_up, weight_down = feedforward_weights()
    branch_grad = (keep * cotangent).astype(jnp.bfloat16)
    branch_grad_all = lax.all_gather(branch_grad, "tensor", axis=0, tiled=True)
    hidden_grad = jnp.dot(branch_grad_all, weight_down, preferred_element_type=jnp.float32)
    grad_down = jnp.einsum(
        "ld,lf->df", branch_grad_all, hidden_ff, preferred_element_type=jnp.float32
    )
    gate_grad = (hidden_grad * upward * sigma * (1.0 + gate * (1.0 - sigma))).astype(jnp.bfloat16)
    up_grad = (hidden_grad * active).astype(jnp.bfloat16)
    grad_gate = jnp.einsum(
        "ld,lf->df", normed_ff_all, gate_grad, preferred_element_type=jnp.float32
    )
    grad_up = jnp.einsum("ld,lf->df", normed_ff_all, up_grad, preferred_element_type=jnp.float32)
    gate_part = jnp.einsum("lf,df->ld", gate_grad, weight_gate, preferred_element_type=jnp.float32)
    up_part = jnp.einsum("lf,df->ld", up_grad, weight_up, preferred_element_type=jnp.float32)
    normed_ff_grad = lax.psum_scatter(
        gate_part + up_part, "tensor", scatter_dimension=0, tiled=True
    )
    grad_gain_two = jnp.sum(normed_ff_grad * unit_two, axis=0)
    scaled_two = normed_ff_grad * gain_two.astype(jnp.float32)
    middle_grad = cotangent + scale_two * (
        scaled_two - unit_two * jnp.mean(scaled_two * unit_two, axis=-1, keepdims=True)
    )
    feedforward_grads = (
        lax.psum_scatter(
            gain_total(grad_gain_two).astype(jnp.bfloat16), "dp", scatter_dimension=0, tiled=True
        ).astype(jnp.float32),
        lax.psum_scatter(
            grad_gate.astype(jnp.bfloat16), "dp", scatter_dimension=0, tiled=True
        ).astype(jnp.float32),
        lax.psum_scatter(
            grad_up.astype(jnp.bfloat16), "dp", scatter_dimension=0, tiled=True
        ).astype(jnp.float32),
        lax.psum_scatter(
            grad_down.astype(jnp.bfloat16), "dp", scatter_dimension=0, tiled=True
        ).astype(jnp.float32),
    )
    gain_one, weight_query, weight_key, weight_value, weight_output = attention_weights()
    attended_grad = (keep * middle_grad).astype(jnp.bfloat16)
    attended_grad_all = lax.all_gather(attended_grad, "tensor", axis=0, tiled=True)
    mixed_grad = jnp.dot(
        attended_grad_all, weight_output, preferred_element_type=jnp.float32
    ).astype(jnp.bfloat16)
    grad_output = jnp.einsum(
        "ld,lc->dc", attended_grad_all, mixed, preferred_element_type=jnp.float32
    )
    mixed_grad_items = (
        mixed_grad.reshape(length, heads_dev, HD).transpose(1, 0, 2).reshape(items, half_len, HD)
    )

    def back_item(carry, operands):
        key_acc, value_acc = carry
        query_block, grad_block, log_total, item = operands
        scores, key_block, value_block = item_scores(query_block, item)
        probs = jnp.exp(scores - log_total[:, None])
        prob_grad = jnp.einsum(
            "rd,md->rm", grad_block, value_block, preferred_element_type=jnp.float32
        )
        score_grad = (
            probs * (prob_grad - jnp.sum(prob_grad * probs, axis=-1, keepdims=True))
        ).astype(jnp.bfloat16)
        query_grad = jnp.dot(score_grad, key_block, preferred_element_type=jnp.float32) * scale
        key_part = (
            jnp.einsum("rm,rd->md", score_grad, query_block, preferred_element_type=jnp.float32)
            * scale
        )
        value_part = jnp.einsum(
            "rm,rd->md", probs.astype(jnp.bfloat16), grad_block, preferred_element_type=jnp.float32
        )
        kv_index = item // 2 // group
        key_acc = key_acc.at[kv_index].add(key_part)
        value_acc = value_acc.at[kv_index].add(value_part)
        return ((key_acc, value_acc), query_grad)

    empty_heads = jnp.zeros((kv_dev, length, HD), jnp.float32)
    (key_acc, value_acc), query_grads = lax.scan(
        back_item, (empty_heads, empty_heads), (query_items, mixed_grad_items, log_totals, item_ids)
    )
    query_rot_grad = query_grads.reshape(heads_dev, length, HD).transpose(1, 0, 2)
    query_raw_grad = (
        rotate_back(query_rot_grad, cosine, sine)
        .astype(jnp.bfloat16)
        .reshape(length, heads_dev * HD)
    )
    key_raw_grad = (
        rotate_back(key_acc.transpose(1, 0, 2), cosine, sine)
        .astype(jnp.bfloat16)
        .reshape(length, kv_dev * HD)
    )
    value_grad = value_acc.transpose(1, 0, 2).astype(jnp.bfloat16).reshape(length, kv_dev * HD)
    grad_query = jnp.einsum(
        "ld,lc->dc", normed_all, query_raw_grad, preferred_element_type=jnp.float32
    )
    grad_key = jnp.einsum("ld,lc->dc", normed_all, key_raw_grad, preferred_element_type=jnp.float32)
    grad_value = jnp.einsum("ld,lc->dc", normed_all, value_grad, preferred_element_type=jnp.float32)
    query_part = jnp.einsum(
        "lc,dc->ld", query_raw_grad, weight_query, preferred_element_type=jnp.float32
    )
    key_part = jnp.einsum("lc,dc->ld", key_raw_grad, weight_key, preferred_element_type=jnp.float32)
    value_part = jnp.einsum(
        "lc,dc->ld", value_grad, weight_value, preferred_element_type=jnp.float32
    )
    normed_grad = lax.psum_scatter(
        (query_part + key_part + value_part).astype(jnp.bfloat16),
        "tensor",
        scatter_dimension=0,
        tiled=True,
    ).astype(jnp.float32)
    grad_gain_one = jnp.sum(normed_grad * unit_one, axis=0)
    scaled_one = normed_grad * gain_one.astype(jnp.float32)
    input_grad = middle_grad + scale_one * (
        scaled_one - unit_one * jnp.mean(scaled_one * unit_one, axis=-1, keepdims=True)
    )
    attention_grads = (
        lax.psum_scatter(
            gain_total(grad_gain_one).astype(jnp.bfloat16), "dp", scatter_dimension=0, tiled=True
        ).astype(jnp.float32),
        lax.psum_scatter(
            grad_query.astype(jnp.bfloat16), "dp", scatter_dimension=0, tiled=True
        ).astype(jnp.float32),
        lax.psum_scatter(
            grad_key.astype(jnp.bfloat16), "dp", scatter_dimension=0, tiled=True
        ).astype(jnp.float32),
        lax.psum_scatter(
            grad_value.astype(jnp.bfloat16), "dp", scatter_dimension=0, tiled=True
        ).astype(jnp.float32),
        lax.psum_scatter(
            grad_output.astype(jnp.bfloat16), "dp", scatter_dimension=0, tiled=True
        ).astype(jnp.float32),
    )
    return (
        layer_out,
        input_grad,
        attention_grads[0],
        attention_grads[1],
        attention_grads[2],
        attention_grads[3],
        attention_grads[4],
        feedforward_grads[0],
        feedforward_grads[1],
        feedforward_grads[2],
        feedforward_grads[3],
    )


def solution(mesh):
    return jax.shard_map(
        body,
        mesh=mesh,
        in_specs=(
            P(("dp", "tensor"), None),
            P(("dp", "tensor")),
            P("dp", None),
            P("dp"),
            P("dp", "tensor"),
            P("dp", "tensor"),
            P("dp", "tensor"),
            P("dp", "tensor"),
            P("dp"),
            P("dp", "tensor"),
            P("dp", "tensor"),
            P("dp", "tensor"),
            P(("dp", "tensor"), None),
        ),
        out_specs=(
            P(("dp", "tensor"), None),
            P(("dp", "tensor"), None),
            P("dp"),
            P("dp", "tensor"),
            P("dp", "tensor"),
            P("dp", "tensor"),
            P("dp", "tensor"),
            P("dp"),
            P("dp", "tensor"),
            P("dp", "tensor"),
            P("dp", "tensor"),
        ),
        check_vma=False,
    )
```

profile of v0, /device:TPU:0, one launch (start us, length us, event | category | flops | bytes accessed | tf_op | source)
XLA Modules:
  0.0 1618.3 jit_solution(11621017453243583606)
XLA Ops:
  7.9 22.2 %all-gather = bf16[8,1,256]{2,1,0:T(2,128)(2,1)S(1)} all-gather(bf16[1,1,256]{2,1,0:T(2,128)(2,1)S(1)} %reshape.568), channel_id=1, replica_groups=mesh['dp'=8,'tensor'=4] {'dp'}, dimensions={0}, use_global_device_ids=true | all-gather | bytes 4608 | tf_op jit(solution)/shard_map/all_gather | solution.py:94
  38.9 31.5 %all_gather.51 = bf16[2048,128]{1,0:T(8,128)(2,1)S(1)} all-gather(bf16[256,128]{1,0:T(8,128)(2,1)S(1)} %copy-done.25), channel_id=1, replica_groups=mesh['dp'=8,'tensor'=4] {'dp'}, dimensions={0}, use_global_device_ids=true | all-gather | bytes 589824 | tf_op jit(solution)/shard_map/all_gather | solution.py:96
  75.4 32.5 %all_gather.52 = bf16[2048,128]{1,0:T(8,128)(2,1)S(1)} all-gather(bf16[256,128]{1,0:T(8,128)(2,1)S(1)} %copy-done.26), channel_id=1, replica_groups=mesh['dp'=8,'tensor'=4] {'dp'}, dimensions={0}, use_global_device_ids=true | all-gather | bytes 589824 | tf_op jit(solution)/shard_map/all_gather | solution.py:97
  114.5 12.2 all-gather.14.cloned.1.call-done
  141.9 72.3 %while.34 = (s32[]{:T(128)}, bf16[8,640,128]{2,1,0:T(8,128)(2,1)}, f32[8,640]{1,0:T(8,128)}, s32[8]{0:T(128)S(1)}, pred[1280,1280]{1,0:T(32,128)(4,1)}, /*index=...) while((s32[]{:T(128)}, bf16[8,640,128]{2,1,0:T(8,128)(2,1)}, ...), condition=%wide.region_16.17_spmd, body=%wide.region_13.16_spmd.sunk | while | flops 426065280 | bytes 11664684 | solution.py:163
  224.1 18.1 %all-gather.1 = bf16[8,1,256]{2,1,0:T(2,128)(2,1)S(1)} all-gather(bf16[1,1,256]{2,1,0:T(2,128)(2,1)S(1)} %reshape.570), channel_id=1, replica_groups=mesh['dp'=8,'tensor'=4] {'dp'}, dimensions={0}, use_global_device_ids=true | all-gather | bytes 4608 | tf_op jit(solution)/shard_map/all_gather | solution.py:103
  242.3 65.2 %reduce-scatter.12.cloned.1.call-done = f32[320,2048]{1,0:T(8,128)} async-done(((f32[1280,2048]{1,0:T(8,128)}), f32[320,2048]{1,0:T(8,128)}) %reduce-scatter.12.cloned.1.call-update) | async-done | bytes 2621456 | tf_op jit(solution)/shard_map/reduce_scatter | solution.py:169
  315.7 86.4 %all-gather.20.cloned.1.call-done = bf16[2048,1408]{1,0:T(8,128)(2,1)} async-done(((bf16[256,1408]{1,0:T(8,128)(2,1)}), bf16[2048,1408]{1,0:T(8,128)(2,1)}) %all-gather.20.cloned.1.call-update) | async-done | bytes 5767184 | tf_op jit(solution)/shard_map/all_gather | solution.py:104
  402.2 40.6 %all-gather.18.cloned.1.call-done = bf16[1280,2048]{1,0:T(8,128)(2,1)} async-done(((bf16[320,2048]{1,0:T(8,128)(2,1)}), bf16[1280,2048]{1,0:T(8,128)(2,1)}) %all-gather.18.cloned.1.call-update) | async-done | bytes 5242896 | tf_op jit(solution)/shard_map/all_gather | solution.py:180
  442.8 13.9 fusion.96
  456.7 81.0 %all-gather.22.cloned.1.call-done = bf16[2048,1408]{1,0:T(8,128)(2,1)} async-done(((bf16[256,1408]{1,0:T(8,128)(2,1)}), bf16[2048,1408]{1,0:T(8,128)(2,1)}) %all-gather.22.cloned.1.call-update) | async-done | bytes 5767184 | tf_op jit(solution)/shard_map/all_gather | solution.py:105
  537.7 13.8 fusion.97
  551.4 79.3 %all-gather.24.cloned.1.call-done = bf16[2048,1408]{1,0:T(8,128)(2,1)} async-done(((bf16[256,1408]{1,0:T(8,128)(2,1)}), bf16[2048,1408]{1,0:T(8,128)(2,1)}) %all-gather.24.cloned.1.call-update) | async-done | bytes 5767184 | tf_op jit(solution)/shard_map/all_gather | solution.py:106
  630.7 40.8 %all-gather.26.cloned.1.call-done = bf16[1280,2048]{1,0:T(8,128)(2,1)} async-done(((bf16[320,2048]{1,0:T(8,128)(2,1)}), bf16[1280,2048]{1,0:T(8,128)(2,1)}) %all-gather.26.cloned.1.call-update) | async-done | bytes 5242896 | tf_op jit(solution)/shard_map/all_gather | solution.py:198
  671.5 19.3 %multiply_convert_fusion.1 = (bf16[1280,1408]{1,0:T(8,128)(2,1)S(1)}, bf16[1280,1408]{1,0:T(8,128)(2,1)}, bf16[1280,1408]{1,0:T(8,128)(2,1)}) fusion(f32[1280,1408]{1,0:T(8,128)} %fusion.96, f32[1280,1408]{1,0:T(8,128)} %fusion.97, bf16[1280,2048]{1,0:T(8,128)(2,1)} %all-gather.26.cloned.1.call-done, bf16[2048,1408]{1,0:T(8,128)(2,1)} %all-gather.24.cloned.1.call-done), kind=kOutput, calls=%fused_computation.56 | convolution fusion | flops 7409008640 | bytes 36241408 | tf_op jit(solution)/shard_map/dot_general | solution.py:199
  690.8 15.1 fusion.98
  705.9 13.2 convolution_add_fusion
  719.1 13.3 convolution_convert_fusion.3
  732.5 72.0 %reduce-scatter.16.cloned.1.call-done = f32[320,2048]{1,0:T(8,128)} async-done(((f32[1280,2048]{1,0:T(8,128)}), f32[320,2048]{1,0:T(8,128)}) %reduce-scatter.16.cloned.1.call-update) | async-done | bytes 2621456 | tf_op jit(solution)/shard_map/reduce_scatter | solution.py:211
  807.5 50.9 %reduce-scatter.14.cloned.1.call-done = bf16[320,2048]{1,0:T(8,128)(2,1)} async-done(((bf16[1280,2048]{1,0:T(8,128)(2,1)}), bf16[320,2048]{1,0:T(8,128)(2,1)}) %reduce-scatter.14.cloned.1.call-update) | async-done | bytes 1310736 | tf_op jit(solution)/shard_map/reduce_scatter | solution.py:186
  863.7 13.0 convolution_convert_fusion.2
  876.8 13.5 convolution_convert_fusion.1
  893.5 13.1 convolution_convert_fusion
  915.2 150.3 %while.35 = (s32[]{:T(128)}, f32[1,1280,128]{2,1,0:T(8,128)}, f32[1,1280,128]{2,1,0:T(8,128)}, f32[8,640,128]{2,1,0:T(8,128)}, s32[8]{0:T(128)S(1)}, /*index=5*/...) while((s32[]{:T(128)}, f32[1,1280,128]{2,1,0:T(8,128)}, ...), condition=%wide.region_25.26_spmd.clone, body=%wide.region_22.25_spmd.clone.sunk | while | flops 1057176960 | bytes 39174844 | solution.py:271
  1134.4 111.4 %reduce-scatter.32.cloned.1.call-done = bf16[256,1408]{1,0:T(8,128)(2,1)} async-done(((bf16[2048,1408]{1,0:T(8,128)(2,1)}), bf16[256,1408]{1,0:T(8,128)(2,1)}) %reduce-scatter.32.cloned.1.call-update) | async-done | bytes 720912 | tf_op jit(solution)/shard_map/reduce_scatter | solution.py:229
  1248.1 63.0 %reduce-scatter.22.cloned.1.call-done = bf16[256,128]{1,0:T(8,128)(2,1)} async-done(((bf16[2048,128]{1,0:T(8,128)(2,1)}), bf16[256,128]{1,0:T(8,128)(2,1)}) %reduce-scatter.22.cloned.1.call-update) | async-done | bytes 65552 | tf_op jit(solution)/shard_map/reduce_scatter | solution.py:316
  1312.6 62.6 %reduce-scatter.24.cloned.1.call-done = bf16[256,128]{1,0:T(8,128)(2,1)} async-done(((bf16[2048,128]{1,0:T(8,128)(2,1)}), bf16[256,128]{1,0:T(8,128)(2,1)}) %reduce-scatter.24.cloned.1.call-update) | async-done | bytes 65552 | tf_op jit(solution)/shard_map/reduce_scatter | solution.py:319
  1376.8 69.7 %reduce-scatter.20.cloned.1.call-done = bf16[256,512]{1,0:T(8,128)(2,1)} async-done(((bf16[2048,512]{1,0:T(8,128)(2,1)}), bf16[256,512]{1,0:T(8,128)(2,1)}) %reduce-scatter.20.cloned.1.call-update) | async-done | bytes 262160 | tf_op jit(solution)/shard_map/reduce_scatter | solution.py:313
  1448.3 69.0 %reduce-scatter.26.cloned.1.call-done = bf16[256,512]{1,0:T(8,128)(2,1)} async-done(((bf16[2048,512]{1,0:T(8,128)(2,1)}), bf16[256,512]{1,0:T(8,128)(2,1)}) %reduce-scatter.26.cloned.1.call-update) | async-done | bytes 262160 | tf_op jit(solution)/shard_map/reduce_scatter | solution.py:322
  1519.0 51.1 %reduce-scatter.18.cloned.1.call-done = bf16[320,2048]{1,0:T(8,128)(2,1)} async-done(((bf16[1280,2048]{1,0:T(8,128)(2,1)}), bf16[320,2048]{1,0:T(8,128)(2,1)}) %reduce-scatter.18.cloned.1.call-update) | async-done | bytes 1310736 | tf_op jit(solution)/shard_map/reduce_scatter | solution.py:298
  1572.9 10.2 all-reduce.2
  1583.0 21.7 %all-reduce.3 = (bf16[2048]{0:T(1024)(128)(2,1)S(1)}, bf16[2048]{0:T(1024)(128)(2,1)S(1)}) all-reduce(bf16[2048]{0:T(1024)(128)(2,1)S(1)} %get-tuple-element.495, bf16[2048]{0:T(1024)(128)(2,1)S(1)} %get-tuple-element.496), channel_id=6, replica_groups=mesh['dp'=8,'tensor'=4] {'dp'}, use_global_device_ids=true, to_apply=%region_30.31.clone | all-reduce | flops 4096 | bytes 16384
  (381 shorter events, 345.5 us)
Async XLA Ops:
  7.2 102.8 %all-gather.12.cloned.1.call-start = ((), (), s32[]{:S(2)}) async-start(), calls=%async_computation.11 | async-start | bytes 6553600 | tf_op jit(solution)/shard_map/all_gather | solution.py:117
  35.2 91.5 %all-gather.14.cloned.1.call-start = ((), (), s32[]{:S(2)}) async-start(), calls=%async_computation.12 | async-start | bytes 2359296 | tf_op jit(solution)/shard_map/all_gather | solution.py:95
  36.0 179.9 %all-gather.16.cloned.1.call-start = ((), (), s32[]{:S(2)}) async-start(), calls=%async_computation.13 | async-start | bytes 2359296 | tf_op jit(solution)/shard_map/all_gather | solution.py:98
  36.7 270.8 %reduce-scatter.12.cloned.1.call-start = ((), (), s32[]{:S(2)}) async-start(), calls=%async_computation.14 | async-start | bytes 13107200 | tf_op jit(solution)/shard_map/reduce_scatter | solution.py:169
  70.4 39.6 %copy-start.9 = (bf16[2048,128]{1,0:T(8,128)(2,1)}, bf16[2048,128]{1,0:T(8,128)(2,1)S(1)}, u32[]{:S(2)}) copy-start(bf16[2048,128]{1,0:T(8,128)(2,1)S(1)} %all_gather.51) | copy-start | bytes 1572868
  223.5 178.7 %all-gather.20.cloned.1.call-start = ((), (), s32[]{:S(2)}) async-start(), calls=%async_computation.16 | async-start | bytes 6488064 | tf_op jit(solution)/shard_map/all_gather | solution.py:104
  224.0 218.8 %all-gather.18.cloned.1.call-start = ((), (), s32[]{:S(2)}) async-start(), calls=%async_computation.15 | async-start | bytes 6553600 | tf_op jit(solution)/shard_map/all_gather | solution.py:180
  242.2 616.2 %copy-start.21 = (f32[8,1,256]{2,1,0:T(1,128)}, f32[8,1,256]{2,1,0:T(1,128)S(1)}, u32[]{:S(2)}) copy-start(f32[8,1,256]{2,1,0:T(1,128)S(1)} %convert_element_type.220) | copy-start | bytes 24580
  311.9 546.6 %copy-start.1 = (f32[320,2048]{1,0:T(8,128)}, f32[320,2048]{1,0:T(8,128)S(1)}, u32[]{:S(2)}) copy-start(f32[320,2048]{1,0:T(8,128)S(1)} %get-tuple-element.500) | copy-start | bytes 7864324
  311.9 546.6 %copy-start.27 = (f32[320]{0:T(512)}, f32[320]{0:T(512)S(1)}, u32[]{:S(2)}) copy-start(f32[320]{0:T(512)S(1)} %add_rsqrt_fusion) | copy-start | bytes 3844
  313.4 224.2 %all-gather.22.cloned.1.call-start = ((), (), s32[]{:S(2)}) async-start(), calls=%async_computation.17 | async-start | bytes 6488064 | tf_op jit(solution)/shard_map/all_gather | solution.py:105
  314.2 316.5 %all-gather.24.cloned.1.call-start = ((), (), s32[]{:S(2)}) async-start(), calls=%async_computation.18 | async-start | bytes 6488064 | tf_op jit(solution)/shard_map/all_gather | solution.py:106
  314.9 356.6 %all-gather.26.cloned.1.call-start = ((), (), s32[]{:S(2)}) async-start(), calls=%async_computation.20 | async-start | bytes 6553600 | tf_op jit(solution)/shard_map/all_gather | solution.py:198
  315.7 488.8 %reduce-scatter.16.cloned.1.call-start = ((), (), s32[]{:S(2)}) async-start(), calls=%async_computation.21 | async-start | bytes 13107200 | tf_op jit(solution)/shard_map/reduce_scatter | solution.py:211
  719.1 139.4 %reduce-scatter.14.cloned.1.call-start = ((), (), s32[]{:S(2)}) async-start(), calls=%async_computation.19 | async-start | bytes 6553600 | tf_op jit(solution)/shard_map/reduce_scatter | solution.py:186
  732.5 174.2 %all-gather.28.cloned.1.call-start = ((), (), s32[]{:S(2)}) async-start(), calls=%async_computation.22 | async-start | bytes 6553600 | tf_op jit(solution)/shard_map/all_gather | solution.py:235
  807.5 56.1 %copy-start.32 = (f32[320]{0:T(512)}, f32[320]{0:T(512)S(1)}, u32[]{:S(2)}) copy-start(f32[320]{0:T(512)S(1)} %broadcast_multiply_fusion.1) | copy-start | bytes 3844
  863.6 256.6 %reduce-scatter.28.cloned.1.call-start = ((), (), s32[]{:S(2)}) async-start(), calls=%async_computation.28 | async-start | bytes 6488064 | tf_op jit(solution)/shard_map/reduce_scatter | solution.py:223
  876.7 255.3 %reduce-scatter.30.cloned.1.call-start = ((), (), s32[]{:S(2)}) async-start(), calls=%async_computation.29 | async-start | bytes 6488064 | tf_op jit(solution)/shard_map/reduce_scatter | solution.py:226
  890.3 355.5 %reduce-scatter.32.cloned.1.call-start = ((), (), s32[]{:S(2)}) async-start(), calls=%async_computation.30 | async-start | bytes 6488064 | tf_op jit(solution)/shard_map/reduce_scatter | solution.py:229
  906.6 404.5 %reduce-scatter.22.cloned.1.call-start = ((), (), s32[]{:S(2)}) async-start(), calls=%async_computation.25 | async-start | bytes 589824 | tf_op jit(solution)/shard_map/reduce_scatter | solution.py:316
  1075.4 299.9 %reduce-scatter.24.cloned.1.call-start = ((), (), s32[]{:S(2)}) async-start(), calls=%async_computation.26 | async-start | bytes 589824 | tf_op jit(solution)/shard_map/reduce_scatter | solution.py:319
  1083.9 362.6 %reduce-scatter.20.cloned.1.call-start = ((), (), s32[]{:S(2)}) async-start(), calls=%async_computation.24 | async-start | bytes 2359296 | tf_op jit(solution)/shard_map/reduce_scatter | solution.py:313
  1095.7 421.6 %reduce-scatter.26.cloned.1.call-start = ((), (), s32[]{:S(2)}) async-start(), calls=%async_computation.27 | async-start | bytes 2359296 | tf_op jit(solution)/shard_map/reduce_scatter | solution.py:322
  1102.8 467.3 %reduce-scatter.18.cloned.1.call-start = ((), (), s32[]{:S(2)}) async-start(), calls=%async_computation.23 | async-start | bytes 6553600 | tf_op jit(solution)/shard_map/reduce_scatter | solution.py:298
  1122.6 447.6 %copy-start.24 = (f32[8,1,256]{2,1,0:T(1,128)S(1)}, f32[8,1,256]{2,1,0:T(1,128)}, u32[]{:S(2)}) copy-start(f32[8,1,256]{2,1,0:T(1,128)} %copy-done.23) | copy-start | bytes 24580
  1122.6 447.6 %copy-start.31 = (f32[320]{0:T(512)S(1)}, f32[320]{0:T(512)}, u32[]{:S(2)}) copy-start(f32[320]{0:T(512)} %copy-done.30) | copy-start | bytes 3844
  1248.1 324.8 %copy-start.29 = (f32[2048]{0:T(1024)S(1)}, f32[2048]{0:T(1024)}, u32[]{:S(2)}) copy-start(f32[2048]{0:T(1024)} %get-tuple-element.453) | copy-start | bytes 24580
  1248.1 357.3 %copy-start.2 = (f32[320,2048]{1,0:T(8,128)S(1)}, f32[320,2048]{1,0:T(8,128)}, u32[]{:S(2)}) copy-start(f32[320,2048]{1,0:T(8,128)} %copy-done.1) | copy-start | bytes 7864324
  1248.1 357.3 %copy-start.22 = (f32[8,1,256]{2,1,0:T(1,128)S(1)}, f32[8,1,256]{2,1,0:T(1,128)}, u32[]{:S(2)}) copy-start(f32[8,1,256]{2,1,0:T(1,128)} %copy-done.21) | copy-start | bytes 24580
  1248.1 357.3 %copy-start.28 = (f32[320]{0:T(512)S(1)}, f32[320]{0:T(512)}, u32[]{:S(2)}) copy-start(f32[320]{0:T(512)} %copy-done.27) | copy-start | bytes 3844
  1248.1 357.3 %copy-start.33 = (f32[320]{0:T(512)S(1)}, f32[320]{0:T(512)}, u32[]{:S(2)}) copy-start(f32[320]{0:T(512)} %copy-done.32) | copy-start | bytes 3844
  (51 other events, 232.3 us)
Sparse Core Ops, SparseCore 0:
  35.3 37.8 all-gather.11
  75.4 51.2 all-gather.13
  128.8 47.7 all-gather.15
  223.6 83.8 reduce-scatter.11
  309.5 92.6 all-gather.19
  404.2 38.6 all-gather.17
  445.0 92.6 all-gather.21
  539.8 90.8 all-gather.23
  632.8 38.6 all-gather.25
  719.2 85.2 reduce-scatter.15
  807.1 51.3 reduce-scatter.13
  863.8 40.4 all-gather.27
  908.3 109.9 reduce-scatter.27
  1022.3 109.7 reduce-scatter.29
  1136.0 109.7 reduce-scatter.31
  1249.3 61.7 reduce-scatter.21
  1314.3 60.9 reduce-scatter.23
  1379.6 66.7 reduce-scatter.19
  1450.4 66.7 reduce-scatter.25
  1519.8 50.3 reduce-scatter.17
where the time goes:
time: 1630 us; the launch traced here: 1620 us
  waiting for transfers between devices  969 us (59%)
  matrix products  330 us (20%)
  blocking collectives  136 us (8%)
  other arithmetic  76.7 us (5%)
  local copies, waits for them, and re-layouts  52.4 us (3%)
  loops' own time  37.5 us (2%)
    reduce_scatter x1, waiting for transfers between devices, body(): lax.psum_scatter(grad_down.astype(jnp.bfloat16), 'dp', scatter_dimension=...  111 us
    all_gather x1, waiting for transfers between devices, feedforward_weights(): lax.all_gather(gate_weight, 'dp', axis=0, tiled=True)  86.4 us
    all_gather x1, waiting for transfers between devices, feedforward_weights(): lax.all_gather(up_weight, 'dp', axis=0, tiled=True)  81 us
    all_gather x1, waiting for transfers between devices, feedforward_weights(): lax.all_gather(down_weight, 'dp', axis=0, tiled=True)  79.3 us
    reduce_scatter x1, waiting for transfers between devices, body(): lax.psum_scatter(gate_part + up_part, 'tensor', scatter_dimension=0, tile...  72 us
    reduce_scatter x1, waiting for transfers between devices, body(): lax.psum_scatter(grad_query.astype(jnp.bfloat16), 'dp', scatter_dimension...  69.7 us
    reduce_scatter x1, waiting for transfers between devices, body(): lax.psum_scatter(grad_output.astype(jnp.bfloat16), 'dp', scatter_dimensio...  69 us
    reduce_scatter x1, waiting for transfers between devices, body(): lax.psum_scatter(jnp.einsum('lc,dc->ld', mixed, weight_output, preferred_...  65.2 us
  transfers between devices with their start and end apart: 20, of which 16 were waited for; matrix products, arithmetic and copies ran while one was open for 23% of the time, Pallas kernels for 0%

commit v1 on v0

--- a/solution.py
+++ b/solution.py
@@ -7,6 +7,32 @@
 HD = 128
 epsilon = 1e-05
 masked_score = -1000000000.0
+
+
+def cut_the_grid(x_local, along_dim):
+    x_local = jnp.moveaxis(x_local, 0, along_dim)
+    far_arr = x_local.shape
+    return x_local.reshape(
+        *far_arr[:along_dim], far_arr[along_dim] * far_arr[along_dim + 1], *far_arr[along_dim + 2 :]
+    )
+
+
+def post_packet(target, peer_axis, row_dim):
+    degree = lax.psum(1, peer_axis)
+    blocks_here = [(tick, (tick + 1) % degree) for tick in range(degree)]
+    stack_in = [(s, dev) for dev, s in blocks_here]
+    known, z = ([], [])
+    for dev_j in range(degree - 1):
+        if dev_j % 2 == 0:
+            current_arr = lax.ppermute(known[-1] if known else target, peer_axis, blocks_here)
+            known.append(current_arr)
+        else:
+            z.append(lax.ppermute(z[-1] if z else target, peer_axis, stack_in))
+    k_now = jnp.stack([*known[::-1], target, *z])
+    b_next = lax.axis_index(peer_axis)
+    arr_now = b_next - len(known)
+    k_now = k_now[(jnp.arange(degree) - arr_now) % degree]
+    return cut_the_grid(k_now, row_dim)
 
 
 def tree_layout(parent_ids):
@@ -102,7 +128,7 @@
         return (
             lax.all_gather(feedforward_gain, "dp", axis=0, tiled=True),
             lax.all_gather(gate_weight, "dp", axis=0, tiled=True),
-            lax.all_gather(up_weight, "dp", axis=0, tiled=True),
+            post_packet(up_weight, "dp", 0),
             lax.all_gather(down_weight, "dp", axis=0, tiled=True),
         )
 

time: 1630 us -> 1630 us (level)
  waiting for transfers between devices: 969 us -> 893 us
  starting transfers between devices: 0.81 us -> 60.2 us
  local copies, waits for them, and re-layouts: 52.4 us -> 73.7 us
    ppermute x0 -> x7, waiting for transfers between devices: none -> 105 us  [the longest x4 102 us: post_packet(): lax.ppermute(known[-1] if known else target, peer_axis, blocks_here)]
    all_gather x1, waiting for transfers between devices: 86.4 us -> 0.01 us  [feedforward_weights(): lax.all_gather(gate_weight, 'dp', axis=0, tiled=True)]
    all_gather x1 -> x0, waiting for transfers between devices: 81 us -> none  [feedforward_weights(): lax.all_gather(up_weight, 'dp', axis=0, tiled=True)]
    ppermute x0 -> x7, starting transfers between devices: none -> 59.4 us  [the longest x3 52.9 us: post_packet(): z.append(lax.ppermute(z[-1] if z else target, peer_axis, stack_in))]
  transfers between devices with their start and end apart: 20 -> 26, of which waited for: 16 -> 19; matrix products, arithmetic and copies ran while one was open for 23% -> 23% of each run, Pallas kernels for 0% -> 0%
where the time goes in v1:
time: 1630 us; the launch traced here: 1620 us
  waiting for transfers between devices  893 us (55%)
  matrix products  326 us (20%)
  blocking collectives  136 us (8%)
  other arithmetic  76.5 us (5%)
  local copies, waits for them, and re-layouts  73.7 us (5%)
  starting transfers between devices  60.2 us (4%)
  loops' own time  37.5 us (2%)
    reduce_scatter x1, waiting for transfers between devices, body(): lax.psum_scatter(grad_down.astype(jnp.bfloat16), 'dp', scatter_dimension=...  111 us
    ppermute x4, waiting for transfers between devices, post_packet(): lax.ppermute(known[-1] if known else target, peer_axis, blocks_here)  102 us
    all_gather x1, waiting for transfers between devices, feedforward_weights(): lax.all_gather(down_weight, 'dp', axis=0, tiled=True)  81.1 us
    reduce_scatter x1, waiting for transfers between devices, body(): lax.psum_scatter(gate_part + up_part, 'tensor', scatter_dimension=0, tile...  72 us
    reduce_scatter x1, waiting for transfers between devices, body(): lax.psum_scatter(grad_query.astype(jnp.bfloat16), 'dp', scatter_dimension...  69.7 us
    reduce_scatter x1, waiting for transfers between devices, body(): lax.psum_scatter(grad_output.astype(jnp.bfloat16), 'dp', scatter_dimensio...  68.7 us
    reduce_scatter x1, waiting for transfers between devices, body(): lax.psum_scatter(jnp.einsum('lc,dc->ld', mixed, weight_output, preferred_...  65.2 us
    reduce_scatter x1, waiting for transfers between devices, body(): lax.psum_scatter(grad_key.astype(jnp.bfloat16), 'dp', scatter_dimension=0...  63 us
  transfers between devices with their start and end apart: 26, of which 19 were waited for; matrix products, arithmetic and copies ran while one was open for 23% of the time, Pallas kernels for 0%

profile of v1, /device:TPU:0, one launch (start us, length us, event | category | flops | bytes accessed | tf_op | source)
XLA Modules:
  0.0 1618.9 jit_solution(5125434262380084777)
XLA Ops:
  7.9 22.2 %all-gather = bf16[8,1,256]{2,1,0:T(2,128)(2,1)S(1)} all-gather(bf16[1,1,256]{2,1,0:T(2,128)(2,1)S(1)} %reshape.630), channel_id=1, replica_groups=mesh['dp'=8,'tensor'=4] {'dp'}, dimensions={0}, use_global_device_ids=true | all-gather | bytes 4608 | tf_op jit(solution)/shard_map/all_gather | solution.py:120
  38.9 31.5 %all_gather.47 = bf16[2048,128]{1,0:T(8,128)(2,1)S(1)} all-gather(bf16[256,128]{1,0:T(8,128)(2,1)S(1)} %copy-done.26), channel_id=1, replica_groups=mesh['dp'=8,'tensor'=4] {'dp'}, dimensions={0}, use_global_device_ids=true | all-gather | bytes 589824 | tf_op jit(solution)/shard_map/all_gather | solution.py:122
  75.4 32.8 %all_gather.48 = bf16[2048,128]{1,0:T(8,128)(2,1)S(1)} all-gather(bf16[256,128]{1,0:T(8,128)(2,1)S(1)} %copy-done.27), channel_id=1, replica_groups=mesh['dp'=8,'tensor'=4] {'dp'}, dimensions={0}, use_global_device_ids=true | all-gather | bytes 589824 | tf_op jit(solution)/shard_map/all_gather | solution.py:123
  141.9 72.3 %while.34 = (s32[]{:T(128)}, bf16[8,640,128]{2,1,0:T(8,128)(2,1)}, f32[8,640]{1,0:T(8,128)}, s32[8]{0:T(128)S(1)}, pred[1280,1280]{1,0:T(32,128)(4,1)}, /*index=...) while((s32[]{:T(128)}, bf16[8,640,128]{2,1,0:T(8,128)(2,1)}, ...), condition=%wide.region_16.17_spmd, body=%wide.region_13.16_spmd.sunk | while | flops 426065280 | bytes 11664684 | solution.py:189
  224.1 18.1 %all-gather.1 = bf16[8,1,256]{2,1,0:T(2,128)(2,1)S(1)} all-gather(bf16[1,1,256]{2,1,0:T(2,128)(2,1)S(1)} %reshape.632), channel_id=1, replica_groups=mesh['dp'=8,'tensor'=4] {'dp'}, dimensions={0}, use_global_device_ids=true | all-gather | bytes 4608 | tf_op jit(solution)/shard_map/all_gather | solution.py:129
  242.3 65.2 %reduce-scatter.12.cloned.1.call-done = f32[320,2048]{1,0:T(8,128)} async-done(((f32[1280,2048]{1,0:T(8,128)}), f32[320,2048]{1,0:T(8,128)}) %reduce-scatter.12.cloned.1.call-update) | async-done | bytes 2621456 | tf_op jit(solution)/shard_map/reduce_scatter | solution.py:195
  315.6 31.5 %collective-permute-done = bf16[256,1408]{1,0:T(8,128)(2,1)} collective-permute-done((bf16[256,1408]{1,0:T(8,128)(2,1)S(1)}, bf16[256,1408]{1,0:T(8,128)(2,1)}, u32[]{:S(2)}, u32[]{:S(2)}) %collective-permute-start) | collective-permute-done | bytes 720928 | tf_op jit(solution)/shard_map/ppermute | solution.py:27
  351.9 37.7 %collective-permute-done.1 = bf16[256,1408]{1,0:T(8,128)(2,1)} collective-permute-done((bf16[256,1408]{1,0:T(8,128)(2,1)}, bf16[256,1408]{1,0:T(8,128)(2,1)}, u32[]{:S(2)}, u32[]{:S(2)}) %collective-permute-start.1) | collective-permute-done | bytes 720928 | tf_op jit(solution)/shard_map/ppermute | solution.py:27
  392.1 30.1 %collective-permute-start.5 = (bf16[256,1408]{1,0:T(8,128)(2,1)}, bf16[256,1408]{1,0:T(8,128)(2,1)}, u32[]{:S(2)}, u32[]{:S(2)}) collective-permute-start(bf16[256,1408]{1,0:T(8,128)(2,1)} %collective-permute-done.4), channel_id=1, source_target_pairs={{4,0},{8,4},{12,8},{16,12},{20,16},{24,20},{28,24},{0,28},{5,1},{9... | collective-permute-start | bytes 2162696 | tf_op jit(solution)/shard_map/ppermute | solution.py:30
  422.1 16.0 collective-permute-done.2
  443.3 18.1 %collective-permute-start.6 = (bf16[256,1408]{1,0:T(8,128)(2,1)}, bf16[256,1408]{1,0:T(8,128)(2,1)S(1)}, u32[]{:S(2)}, u32[]{:S(2)}) collective-permute-start(bf16[256,1408]{1,0:T(8,128)(2,1)} %collective-permute-done.5), channel_id=1, source_target_pairs={{4,0},{8,4},{12,8},{16,12},{20,16},{24,20},{28,24},{0,28},{5,1},{9... | collective-permute-start | bytes 2162696 | tf_op jit(solution)/shard_map/ppermute | solution.py:30
  461.4 17.2 %collective-permute-done.3 = bf16[256,1408]{1,0:T(8,128)(2,1)} collective-permute-done((bf16[256,1408]{1,0:T(8,128)(2,1)}, bf16[256,1408]{1,0:T(8,128)(2,1)}, u32[]{:S(2)}, u32[]{:S(2)}) %collective-permute-start.3) | collective-permute-done | bytes 720928 | tf_op jit(solution)/shard_map/ppermute | solution.py:27
  499.8 26.7 %all-gather.17.cloned.1.call-done = bf16[1280,2048]{1,0:T(8,128)(2,1)} async-done(((bf16[320,2048]{1,0:T(8,128)(2,1)}), bf16[1280,2048]{1,0:T(8,128)(2,1)}) %all-gather.17.cloned.1.call-update) | async-done | bytes 5242896 | tf_op jit(solution)/shard_map/all_gather | solution.py:206
  526.5 13.8 fusion.98
  540.2 81.1 %all-gather.21.cloned.1.call-done = bf16[2048,1408]{1,0:T(8,128)(2,1)} async-done(((bf16[256,1408]{1,0:T(8,128)(2,1)}), bf16[2048,1408]{1,0:T(8,128)(2,1)}) %all-gather.21.cloned.1.call-update) | async-done | bytes 5767184 | tf_op jit(solution)/shard_map/all_gather | solution.py:132
  621.3 40.8 %all-gather.23.cloned.1.call-done = bf16[1280,2048]{1,0:T(8,128)(2,1)} async-done(((bf16[320,2048]{1,0:T(8,128)(2,1)}), bf16[1280,2048]{1,0:T(8,128)(2,1)}) %all-gather.23.cloned.1.call-update) | async-done | bytes 5242896 | tf_op jit(solution)/shard_map/all_gather | solution.py:224
  662.1 13.9 fusion.99
  676.0 17.0 %multiply_convert_fusion.1 = (bf16[1280,1408]{1,0:T(8,128)(2,1)}, bf16[1280,1408]{1,0:T(8,128)(2,1)}, bf16[1280,1408]{1,0:T(8,128)(2,1)}) fusion(f32[1280,1408]{1,0:T(8,128)} %fusion.99, f32[1280,1408]{1,0:T(8,128)} %fusion.98, bf16[1280,2048]{1,0:T(8,128)(2,1)S(1)} %copy-done.36, bf16[2048,1408]{1,0:T(8,128)(2,1)} %bitcast.223), kind=kOutput, calls=%fused_computation.57 | convolution fusion | flops 7409008640 | bytes 36241408 | tf_op jit(solution)/shard_map/dot_general | solution.py:208
  692.9 14.0 fusion.100
  706.9 13.2 convolution_add_fusion
  720.2 13.3 convolution_convert_fusion.3
  733.6 72.0 %reduce-scatter.16.cloned.1.call-done = f32[320,2048]{1,0:T(8,128)} async-done(((f32[1280,2048]{1,0:T(8,128)}), f32[320,2048]{1,0:T(8,128)}) %reduce-scatter.16.cloned.1.call-update) | async-done | bytes 2621456 | tf_op jit(solution)/shard_map/reduce_scatter | solution.py:237
  808.6 50.8 %reduce-scatter.14.cloned.1.call-done = bf16[320,2048]{1,0:T(8,128)(2,1)} async-done(((bf16[1280,2048]{1,0:T(8,128)(2,1)}), bf16[320,2048]{1,0:T(8,128)(2,1)}) %reduce-scatter.14.cloned.1.call-update) | async-done | bytes 1310736 | tf_op jit(solution)/shard_map/reduce_scatter | solution.py:212
  877.7 13.5 convolution_convert_fusion.1
  916.2 150.1 %while.35 = (s32[]{:T(128)}, f32[1,1280,128]{2,1,0:T(8,128)}, f32[1,1280,128]{2,1,0:T(8,128)}, f32[8,640,128]{2,1,0:T(8,128)}, s32[8]{0:T(128)S(1)}, /*index=5*/...) while((s32[]{:T(128)}, f32[1,1280,128]{2,1,0:T(8,128)}, ...), condition=%wide.region_25.26_spmd.clone, body=%wide.region_22.25_spmd.clone.sunk | while | flops 1057176960 | bytes 39174844 | solution.py:297
  1135.4 111.4 %reduce-scatter.32.cloned.1.call-done = bf16[256,1408]{1,0:T(8,128)(2,1)} async-done(((bf16[2048,1408]{1,0:T(8,128)(2,1)}), bf16[256,1408]{1,0:T(8,128)(2,1)}) %reduce-scatter.32.cloned.1.call-update) | async-done | bytes 720912 | tf_op jit(solution)/shard_map/reduce_scatter | solution.py:255
  1249.1 63.0 %reduce-scatter.22.cloned.1.call-done = bf16[256,128]{1,0:T(8,128)(2,1)} async-done(((bf16[2048,128]{1,0:T(8,128)(2,1)}), bf16[256,128]{1,0:T(8,128)(2,1)}) %reduce-scatter.22.cloned.1.call-update) | async-done | bytes 65552 | tf_op jit(solution)/shard_map/reduce_scatter | solution.py:342
  1313.6 62.7 %reduce-scatter.24.cloned.1.call-done = bf16[256,128]{1,0:T(8,128)(2,1)} async-done(((bf16[2048,128]{1,0:T(8,128)(2,1)}), bf16[256,128]{1,0:T(8,128)(2,1)}) %reduce-scatter.24.cloned.1.call-update) | async-done | bytes 65552 | tf_op jit(solution)/shard_map/reduce_scatter | solution.py:345
  1377.8 69.7 %reduce-scatter.20.cloned.1.call-done = bf16[256,512]{1,0:T(8,128)(2,1)} async-done(((bf16[2048,512]{1,0:T(8,128)(2,1)}), bf16[256,512]{1,0:T(8,128)(2,1)}) %reduce-scatter.20.cloned.1.call-update) | async-done | bytes 262160 | tf_op jit(solution)/shard_map/reduce_scatter | solution.py:339
  1449.3 68.7 %reduce-scatter.26.cloned.1.call-done = bf16[256,512]{1,0:T(8,128)(2,1)} async-done(((bf16[2048,512]{1,0:T(8,128)(2,1)}), bf16[256,512]{1,0:T(8,128)(2,1)}) %reduce-scatter.26.cloned.1.call-update) | async-done | bytes 262160 | tf_op jit(solution)/shard_map/reduce_scatter | solution.py:348
  1519.7 51.3 %reduce-scatter.18.cloned.1.call-done = bf16[320,2048]{1,0:T(8,128)(2,1)} async-done(((bf16[1280,2048]{1,0:T(8,128)(2,1)}), bf16[320,2048]{1,0:T(8,128)(2,1)}) %reduce-scatter.18.cloned.1.call-update) | async-done | bytes 1310736 | tf_op jit(solution)/shard_map/reduce_scatter | solution.py:324
  1583.9 21.7 %all-reduce.3 = (bf16[2048]{0:T(1024)(128)(2,1)S(1)}, bf16[2048]{0:T(1024)(128)(2,1)S(1)}) all-reduce(bf16[2048]{0:T(1024)(128)(2,1)S(1)} %get-tuple-element.495, bf16[2048]{0:T(1024)(128)(2,1)S(1)} %get-tuple-element.496), channel_id=6, replica_groups=mesh['dp'=8,'tensor'=4] {'dp'}, use_global_device_ids=true, to_apply=%region_30.31.clone | all-reduce | flops 4096 | bytes 16384
  (410 shorter events, 427.4 us)
Async XLA Ops:
  7.2 103.0 %all-gather.11.cloned.1.call-start = ((), (), s32[]{:S(2)}) async-start(), calls=%async_computation.11 | async-start | bytes 6553600 | tf_op jit(solution)/shard_map/all_gather | solution.py:143
  35.2 91.5 %all-gather.13.cloned.1.call-start = ((), (), s32[]{:S(2)}) async-start(), calls=%async_computation.12 | async-start | bytes 2359296 | tf_op jit(solution)/shard_map/all_gather | solution.py:121
  36.0 179.8 %all-gather.15.cloned.1.call-start = ((), (), s32[]{:S(2)}) async-start(), calls=%async_computation.13 | async-start | bytes 2359296 | tf_op jit(solution)/shard_map/all_gather | solution.py:124
  36.7 270.8 %reduce-scatter.12.cloned.1.call-start = ((), (), s32[]{:S(2)}) async-start(), calls=%async_computation.14 | async-start | bytes 13107200 | tf_op jit(solution)/shard_map/reduce_scatter | solution.py:195
  223.5 276.3 %all-gather.19.cloned.1.call-start = ((), (), s32[]{:S(2)}) async-start(), calls=%async_computation.16 | async-start | bytes 6488064 | tf_op jit(solution)/shard_map/all_gather | solution.py:130
  224.1 302.4 %all-gather.17.cloned.1.call-start = ((), (), s32[]{:S(2)}) async-start(), calls=%async_computation.15 | async-start | bytes 6553600 | tf_op jit(solution)/shard_map/all_gather | solution.py:206
  242.3 617.1 %copy-start.22 = (f32[8,1,256]{2,1,0:T(1,128)}, f32[8,1,256]{2,1,0:T(1,128)S(1)}, u32[]{:S(2)}) copy-start(f32[8,1,256]{2,1,0:T(1,128)S(1)} %convert_element_type.220) | copy-start | bytes 24580
  311.9 547.6 %copy-start.1 = (f32[320,2048]{1,0:T(8,128)}, f32[320,2048]{1,0:T(8,128)S(1)}, u32[]{:S(2)}) copy-start(f32[320,2048]{1,0:T(8,128)S(1)} %get-tuple-element.500) | copy-start | bytes 7864324
  311.9 547.6 %copy-start.28 = (f32[320]{0:T(512)}, f32[320]{0:T(512)S(1)}, u32[]{:S(2)}) copy-start(f32[320]{0:T(512)S(1)} %add_rsqrt_fusion) | copy-start | bytes 3844
  313.3 308.1 %all-gather.21.cloned.1.call-start = ((), (), s32[]{:S(2)}) async-start(), calls=%async_computation.17 | async-start | bytes 6488064 | tf_op jit(solution)/shard_map/all_gather | solution.py:132
  314.0 348.1 %all-gather.23.cloned.1.call-start = ((), (), s32[]{:S(2)}) async-start(), calls=%async_computation.19 | async-start | bytes 6553600 | tf_op jit(solution)/shard_map/all_gather | solution.py:224
  314.1 33.0 %collective-permute-start = (bf16[256,1408]{1,0:T(8,128)(2,1)S(1)}, bf16[256,1408]{1,0:T(8,128)(2,1)}, u32[]{:S(2)}, u32[]{:S(2)}) collective-permute-start(bf16[256,1408]{1,0:T(8,128)(2,1)S(1)} %copy-done.21), channel_id=1, source_target_pairs={{0,4},{4,8},{8,12},{12,16},{16,20},{20,24},{24,28},{28,0},{1,5},{5... | collective-permute-start | bytes 2162696 | tf_op jit(solution)/shard_map/ppermute | solution.py:27
  347.1 42.5 %collective-permute-start.1 = (bf16[256,1408]{1,0:T(8,128)(2,1)}, bf16[256,1408]{1,0:T(8,128)(2,1)}, u32[]{:S(2)}, u32[]{:S(2)}) collective-permute-start(bf16[256,1408]{1,0:T(8,128)(2,1)} %collective-permute-done), channel_id=1, source_target_pairs={{0,4},{4,8},{8,12},{12,16},{16,20},{20,24},{24,28},{28,0},{1,5},{5... | collective-permute-start | bytes 2162696 | tf_op jit(solution)/shard_map/ppermute | solution.py:27
  347.1 458.5 %reduce-scatter.16.cloned.1.call-start = ((), (), s32[]{:S(2)}) async-start(), calls=%async_computation.20 | async-start | bytes 13107200 | tf_op jit(solution)/shard_map/reduce_scatter | solution.py:237
  347.1 44.9 %collective-permute-start.4 = (bf16[256,1408]{1,0:T(8,128)(2,1)S(1)}, bf16[256,1408]{1,0:T(8,128)(2,1)}, u32[]{:S(2)}, u32[]{:S(2)}) collective-permute-start(bf16[256,1408]{1,0:T(8,128)(2,1)S(1)} %copy-done.21), channel_id=1, source_target_pairs={{4,0},{8,4},{12,8},{16,12},{20,16},{24,20},{28,24},{0,28},{5,1},{9... | collective-permute-start | bytes 2162696 | tf_op jit(solution)/shard_map/ppermute | solution.py:30
  389.6 48.5 %collective-permute-start.2 = (bf16[256,1408]{1,0:T(8,128)(2,1)}, bf16[256,1408]{1,0:T(8,128)(2,1)}, u32[]{:S(2)}, u32[]{:S(2)}) collective-permute-start(bf16[256,1408]{1,0:T(8,128)(2,1)} %collective-permute-done.1), channel_id=1, source_target_pairs={{0,4},{4,8},{8,12},{12,16},{16,20},{20,24},{24,28},{28,0},{1,5},{5... | collective-permute-start | bytes 2162696 | tf_op jit(solution)/shard_map/ppermute | solution.py:27
  392.1 51.2 %collective-permute-start.5 = (bf16[256,1408]{1,0:T(8,128)(2,1)}, bf16[256,1408]{1,0:T(8,128)(2,1)}, u32[]{:S(2)}, u32[]{:S(2)}) collective-permute-start(bf16[256,1408]{1,0:T(8,128)(2,1)} %collective-permute-done.4), channel_id=1, source_target_pairs={{4,0},{8,4},{12,8},{16,12},{20,16},{24,20},{28,24},{0,28},{5,1},{9... | collective-permute-start | bytes 2162696 | tf_op jit(solution)/shard_map/ppermute | solution.py:30
  438.1 40.5 %collective-permute-start.3 = (bf16[256,1408]{1,0:T(8,128)(2,1)}, bf16[256,1408]{1,0:T(8,128)(2,1)}, u32[]{:S(2)}, u32[]{:S(2)}) collective-permute-start(bf16[256,1408]{1,0:T(8,128)(2,1)} %collective-permute-done.2), channel_id=1, source_target_pairs={{0,4},{4,8},{8,12},{12,16},{16,20},{20,24},{24,28},{28,0},{1,5},{5... | collective-permute-start | bytes 2162696 | tf_op jit(solution)/shard_map/ppermute | solution.py:27
  443.3 48.4 %collective-permute-start.6 = (bf16[256,1408]{1,0:T(8,128)(2,1)}, bf16[256,1408]{1,0:T(8,128)(2,1)S(1)}, u32[]{:S(2)}, u32[]{:S(2)}) collective-permute-start(bf16[256,1408]{1,0:T(8,128)(2,1)} %collective-permute-done.5), channel_id=1, source_target_pairs={{4,0},{8,4},{12,8},{16,12},{20,16},{24,20},{28,24},{0,28},{5,1},{9... | collective-permute-start | bytes 2162696 | tf_op jit(solution)/shard_map/ppermute | solution.py:30
  720.1 139.3 %reduce-scatter.14.cloned.1.call-start = ((), (), s32[]{:S(2)}) async-start(), calls=%async_computation.18 | async-start | bytes 6553600 | tf_op jit(solution)/shard_map/reduce_scatter | solution.py:212
  733.5 174.1 %all-gather.25.cloned.1.call-start = ((), (), s32[]{:S(2)}) async-start(), calls=%async_computation.21 | async-start | bytes 6553600 | tf_op jit(solution)/shard_map/all_gather | solution.py:261
  864.6 256.5 %reduce-scatter.28.cloned.1.call-start = ((), (), s32[]{:S(2)}) async-start(), calls=%async_computation.27 | async-start | bytes 6488064 | tf_op jit(solution)/shard_map/reduce_scatter | solution.py:249
  877.6 255.4 %reduce-scatter.30.cloned.1.call-start = ((), (), s32[]{:S(2)}) async-start(), calls=%async_computation.28 | async-start | bytes 6488064 | tf_op jit(solution)/shard_map/reduce_scatter | solution.py:252
  891.2 355.5 %reduce-scatter.32.cloned.1.call-start = ((), (), s32[]{:S(2)}) async-start(), calls=%async_computation.29 | async-start | bytes 6488064 | tf_op jit(solution)/shard_map/reduce_scatter | solution.py:255
  907.6 404.6 %reduce-scatter.22.cloned.1.call-start = ((), (), s32[]{:S(2)}) async-start(), calls=%async_computation.24 | async-start | bytes 589824 | tf_op jit(solution)/shard_map/reduce_scatter | solution.py:342
  1076.1 300.2 %reduce-scatter.24.cloned.1.call-start = ((), (), s32[]{:S(2)}) async-start(), calls=%async_computation.25 | async-start | bytes 589824 | tf_op jit(solution)/shard_map/reduce_scatter | solution.py:345
  1084.6 362.9 %reduce-scatter.20.cloned.1.call-start = ((), (), s32[]{:S(2)}) async-start(), calls=%async_computation.23 | async-start | bytes 2359296 | tf_op jit(solution)/shard_map/reduce_scatter | solution.py:339
  1096.4 421.5 %reduce-scatter.26.cloned.1.call-start = ((), (), s32[]{:S(2)}) async-start(), calls=%async_computation.26 | async-start | bytes 2359296 | tf_op jit(solution)/shard_map/reduce_scatter | solution.py:348
  1103.6 467.4 %reduce-scatter.18.cloned.1.call-start = ((), (), s32[]{:S(2)}) async-start(), calls=%async_computation.22 | async-start | bytes 6553600 | tf_op jit(solution)/shard_map/reduce_scatter | solution.py:324
  1123.4 447.6 %copy-start.25 = (f32[8,1,256]{2,1,0:T(1,128)S(1)}, f32[8,1,256]{2,1,0:T(1,128)}, u32[]{:S(2)}) copy-start(f32[8,1,256]{2,1,0:T(1,128)} %copy-done.24) | copy-start | bytes 24580
  1123.4 447.6 %copy-start.32 = (f32[320]{0:T(512)S(1)}, f32[320]{0:T(512)}, u32[]{:S(2)}) copy-start(f32[320]{0:T(512)} %copy-done.31) | copy-start | bytes 3844
  1249.1 357.2 %copy-start.34 = (f32[320]{0:T(512)S(1)}, f32[320]{0:T(512)}, u32[]{:S(2)}) copy-start(f32[320]{0:T(512)} %copy-done.33) | copy-start | bytes 3844
  (60 other events, 1799.6 us)
Sparse Core Ops, SparseCore 0:
  35.3 37.8 all-gather.10
  75.4 51.2 all-gather.12
  128.8 47.7 all-gather.14
  223.6 83.8 reduce-scatter.11
  309.5 169.1 all-gather.18
  480.7 45.7 all-gather.16
  528.6 92.6 all-gather.20
  623.5 38.6 all-gather.22
  720.3 85.2 reduce-scatter.15
  808.0 51.3 reduce-scatter.13
  864.7 40.4 all-gather.24
  909.1 109.9 reduce-scatter.27
  1023.2 109.7 reduce-scatter.29
  1137.0 109.7 reduce-scatter.31
  1250.3 61.7 reduce-scatter.21
  1315.3 60.9 reduce-scatter.23
  1380.6 66.7 reduce-scatter.19
  1451.3 66.6 reduce-scatter.25
  1520.6 50.3 reduce-scatter.17
